TPU v7x, 256 devices: a whole 4x4x8 slice. The times are simulated.
256 devices in a mesh: section: 4 (over x), shard: 64 (over z, y, core).
Axes of the slice: x: 4, y: 4, z: 8, core: 2. Of those that a mesh axis runs over, the one named last changes fastest.
Arguments:
- features: bfloat16 [4096, 768], P('shard'), may hold values from -6 to 6
- tile_cols: int32 [4, 32, 16], P('section'), may hold values from 0 to 31
- live_tiles: int32 [4, 32], P('section'), may hold values from 1 to 16, 256 in all within a row
- tile_values: bfloat16 [4, 4096, 16, 128], P('section', 'shard'), may hold values from -0.375 to 0.375
- degrees: int32 [4, 4096], P('section', 'shard'), may hold values from 1 to 8
Outputs:
- hops: bfloat16 [4, 4096, 768], P('section', 'shard')
Inputs may be any that keep to these rules, and one draw needn't show every extreme that they name: `live_tiles`: every row block has at least one live tile slot; the live counts of one relation sum to 256.
All inputs are finite; a program needn't handle non-finite values.
Results may differ from a plain program's by a relative error of at most 0.0056.
Values may be sent and summed in bfloat16 or wider, within the bound.
A program may use at most 64 MiB of HBM per device.

v0:
```python
import jax
import jax.numpy as jnp
from jax import lax
from jax.sharding import PartitionSpec as P


def from_behind(value, axis, by):
    peers = lax.axis_size(axis)
    pairs = [(i, i + by) for i in range(peers) if 0 <= i + by < peers]
    return lax.ppermute(value, axis, pairs)


def propagate(gathered, block_ids, live_count, tile_rows, row_scale):
    tile_size = tile_rows.shape[2]
    width = gathered.shape[1]
    blocks = gathered.reshape(gathered.shape[0] // tile_size, tile_size, width)
    source = blocks[block_ids]
    live_mask = (jnp.arange(tile_rows.shape[1], dtype=jnp.int32) < live_count).astype(jnp.bfloat16)
    masked = tile_rows * live_mask[None, :, None]
    summed = jnp.einsum("rkc,kcw->rw", masked, source, preferred_element_type=jnp.float32)
    return (summed * row_scale[:, None]).astype(jnp.bfloat16)


def per_device(features, tile_cols, live_tiles, tile_values, degrees):
    section_index = lax.axis_index("section")
    section_count = lax.axis_size("section")
    tile_rows = tile_values[0]
    row_count = tile_rows.shape[0]
    tile_size = tile_rows.shape[2]
    block_row = lax.axis_index("shard") * row_count // tile_size
    block_ids = lax.dynamic_index_in_dim(tile_cols[0], block_row, 0, keepdims=False)
    live_count = lax.dynamic_index_in_dim(live_tiles[0], block_row, 0, keepdims=False)
    row_scale = lax.rsqrt(degrees[0].astype(jnp.float32))
    width = features.shape[1]
    result = jnp.zeros((row_count, width), jnp.bfloat16)
    arrived = jnp.zeros((row_count, width), jnp.bfloat16)
    for hop_num in range(section_count):
        slab_in = jnp.where(section_index == 0, features, arrived)
        gathered = lax.all_gather(slab_in, "shard", axis=0, tiled=True)
        output = propagate(gathered, block_ids, live_count, tile_rows, row_scale)
        result = jnp.where(section_index == hop_num, output, result)
        arrived = from_behind(output, "section", 1)
    return result[None]


def solution(mesh):
    in_specs = (
        P("shard", None),
        P("section", None, None),
        P("section", None),
        P("section", "shard", None, None),
        P("section", "shard"),
    )
    out_specs = P("section", "shard", None)
    return jax.shard_map(
        per_device, mesh=mesh, in_specs=in_specs, out_specs=out_specs, check_vma=False
    )
```

profile of v0, /device:TPU:3, one launch (start us, length us, event | category | flops | bytes accessed | tf_op | source)
XLA Modules:
  0.0 375.5 jit_solution(7608889095608387722)
XLA Ops:
  6.5 0.0 copy-start
  6.5 0.0 all-gather.5.cloned.1.call-start
  6.5 0.7 broadcast_select_fusion.3
  7.2 0.1 all-gather.5.cloned.1.call-update
  7.3 0.0 all-gather.7.cloned.1.call-start
  7.3 1.3 constant_dynamic-slice_fusion
  8.6 0.0 copy-done
  8.6 0.2 dynamic-slice_reduce_fusion
  8.8 0.6 compare_convert_fusion
  9.5 0.7 rsqrt_bitcast_fusion
  10.1 1.0 bitcast_multiply_fusion
  11.2 82.9 %all-gather.5.cloned.1.call-done = bf16[4096,768]{1,0:T(8,128)(2,1)} async-done(((bf16[64,768]{1,0:T(8,128)(2,1)}), bf16[4096,768]{1,0:T(8,128)(2,1)}) %all-gather.5.cloned.1.call-update) | async-done | bytes 6291472 | tf_op jit(solution)/shard_map/all_gather | solution.py:39
  94.0 3.5 gather_fusion
  97.6 0.0 copy-start.1
  97.6 0.7 fusion.4
  98.3 0.0 copy-start.2
  98.3 0.6 copy-done.2
  98.9 3.1 collective-permute-start
  102.0 2.9 collective-permute-done
  104.9 0.0 copy-done.1
  104.9 0.7 broadcast_select_fusion.2
  105.5 0.0 all-gather.7.cloned.1.call-update
  105.5 0.0 all-gather.9.cloned.1.call-start
  105.6 78.2 %all-gather.7.cloned.1.call-done = bf16[4096,768]{1,0:T(8,128)(2,1)} async-done(((bf16[64,768]{1,0:T(8,128)(2,1)}), bf16[4096,768]{1,0:T(8,128)(2,1)}) %all-gather.7.cloned.1.call-update) | async-done | bytes 6291472 | tf_op jit(solution)/shard_map/all_gather | solution.py:39
  183.8 3.5 gather_fusion.1
  187.3 0.7 fusion.5
  188.0 0.0 copy-start.4
  188.0 0.6 copy-done.4
  188.6 3.1 collective-permute-start.1
  191.7 2.9 collective-permute-done.1
  194.6 0.7 broadcast_select_fusion.1
  195.2 0.0 all-gather.9.cloned.1.call-update
  195.2 0.0 all-gather.11.cloned.1.call-start
  195.3 78.2 %all-gather.9.cloned.1.call-done = bf16[4096,768]{1,0:T(8,128)(2,1)} async-done(((bf16[64,768]{1,0:T(8,128)(2,1)}), bf16[4096,768]{1,0:T(8,128)(2,1)}) %all-gather.9.cloned.1.call-update) | async-done | bytes 6291472 | tf_op jit(solution)/shard_map/all_gather | solution.py:39
  273.5 3.5 gather_fusion.2
  277.0 0.7 fusion.6
  277.7 0.0 copy-start.5
  277.7 0.6 copy-done.5
  278.3 3.1 collective-permute-start.2
  281.4 2.9 collective-permute-done.2
  284.3 0.7 broadcast_select_fusion
  284.9 0.0 all-gather.11.cloned.1.call-update
  285.0 78.2 %all-gather.11.cloned.1.call-done = bf16[4096,768]{1,0:T(8,128)(2,1)} async-done(((bf16[64,768]{1,0:T(8,128)(2,1)}), bf16[4096,768]{1,0:T(8,128)(2,1)}) %all-gather.11.cloned.1.call-update) | async-done | bytes 6291472 | tf_op jit(solution)/shard_map/all_gather | solution.py:39
  363.2 0.0 copy-start.3
  363.2 3.6 gather_fusion.3
  366.7 0.0 copy-done.3
  366.7 2.2 fusion.9
  (2 shorter events, 0.0 us)
Async XLA Ops:
  6.5 2.1 copy-start
  6.5 87.5 %all-gather.5.cloned.1.call-start = ((), (), s32[]{:S(2)}) async-start(), calls=%async_computation | async-start | bytes 6389760 | tf_op jit(solution)/shard_map/all_gather | solution.py:39
  7.3 176.5 %all-gather.7.cloned.1.call-start = ((), (), s32[]{:S(2)}) async-start(), calls=%async_computation.1 | async-start | bytes 6389760 | tf_op jit(solution)/shard_map/all_gather | solution.py:39
  97.6 7.3 %copy-start.1 = (bf16[64,768]{1,0:T(8,128)(2,1)S(1)}, bf16[64,768]{1,0:T(8,128)(2,1)}, u32[]{:S(2)}) copy-start(bf16[64,768]{1,0:T(8,128)(2,1)} %param.5) | copy-start | bytes 294916
  98.3 0.6 copy-start.2
  98.9 6.0 %collective-permute-start = (bf16[64,768]{1,0:T(8,128)(2,1)S(1)}, bf16[64,768]{1,0:T(8,128)(2,1)S(1)}, u32[]{:S(2)}, u32[]{:S(2)}) collective-permute-start(bf16[64,768]{1,0:T(8,128)(2,1)S(1)} %fusion.4), channel_id=1, source_target_pairs={{0,64},{64,128},{128,192},{1,65},{65,129},{129,193},{2,66},{66,130... | collective-permute-start | bytes 294920 | tf_op jit(solution)/shard_map/ppermute | solution.py:10
  105.5 167.9 %all-gather.9.cloned.1.call-start = ((), (), s32[]{:S(2)}) async-start(), calls=%async_computation.2 | async-start | bytes 6389760 | tf_op jit(solution)/shard_map/all_gather | solution.py:39
  188.0 0.6 copy-start.4
  188.6 6.0 %collective-permute-start.1 = (bf16[64,768]{1,0:T(8,128)(2,1)S(1)}, bf16[64,768]{1,0:T(8,128)(2,1)S(1)}, u32[]{:S(2)}, u32[]{:S(2)}) collective-permute-start(bf16[64,768]{1,0:T(8,128)(2,1)S(1)} %fusion.5), channel_id=1, source_target_pairs={{0,64},{64,128},{128,192},{1,65},{65,129},{129,193},{2,66},{66,130... | collective-permute-start | bytes 294920 | tf_op jit(solution)/shard_map/ppermute | solution.py:10
  195.2 167.9 %all-gather.11.cloned.1.call-start = ((), (), s32[]{:S(2)}) async-start(), calls=%async_computation.3 | async-start | bytes 6389760 | tf_op jit(solution)/shard_map/all_gather | solution.py:39
  277.7 0.6 copy-start.5
  278.3 6.0 %collective-permute-start.2 = (bf16[64,768]{1,0:T(8,128)(2,1)S(1)}, bf16[64,768]{1,0:T(8,128)(2,1)S(1)}, u32[]{:S(2)}, u32[]{:S(2)}) collective-permute-start(bf16[64,768]{1,0:T(8,128)(2,1)S(1)} %fusion.6), channel_id=1, source_target_pairs={{0,64},{64,128},{128,192},{1,65},{65,129},{129,193},{2,66},{66,130... | collective-permute-start | bytes 294920 | tf_op jit(solution)/shard_map/ppermute | solution.py:10
  363.2 3.6 copy-start.3
Sparse Core Ops, SparseCore 0:
  10.1 83.9 all-gather.4
  105.7 78.0 all-gather.6
  195.4 78.0 all-gather.8
  285.1 78.0 all-gather.10
where the time goes:
time: 376 us; the launch traced here: 375 us
  waiting for transfers between devices  326 us (87%)
  local copies, waits for them, and re-layouts  17.5 us (5%)
  between operations  13.3 us (4%)
  starting transfers between devices  9.37 us (2%)
  other arithmetic  4.97 us (1%)
  matrix products  4.2 us (1%)
    all_gather x4, waiting for transfers between devices, per_device(): gathered = lax.all_gather(slab_in, 'shard', axis=0, tiled=True)  317 us
    gather x4, local copies, waits for them, and re-layouts, propagate(): source = blocks[block_ids]  14.2 us
    ppermute x3, starting transfers between devices, from_behind(): return lax.ppermute(value, axis, pairs)  9.25 us
    ppermute x3, waiting for transfers between devices, from_behind(): return lax.ppermute(value, axis, pairs)  8.62 us
  transfers between devices with their start and end apart: 7, of which 7 were waited for; matrix products, arithmetic and copies ran while one was open for 1% of the time, Pallas kernels for 0%

commit v1 on v0

--- a/solution.py
+++ b/solution.py
@@ -36,7 +36,10 @@
     arrived = jnp.zeros((row_count, width), jnp.bfloat16)
     for hop_num in range(section_count):
         slab_in = jnp.where(section_index == 0, features, arrived)
-        gathered = lax.all_gather(slab_in, "shard", axis=0, tiled=True)
+        y_new = lax.axis_size("shard")
+        z2 = jnp.stack([slab_in] * y_new, axis=0)
+        shaped = lax.all_to_all(z2, "shard", 0, 0)
+        gathered = jnp.concatenate(shaped, 0)
         output = propagate(gathered, block_ids, live_count, tile_rows, row_scale)
         result = jnp.where(section_index == hop_num, output, result)
         arrived = from_behind(output, "section", 1)

time: 376 us -> 641 us (1.70)
  blocking collectives: 0 us -> 296 us
  waiting for transfers between devices: 326 us -> 283 us
  starting transfers between devices: 9.37 us -> 30.3 us
  between operations: 13.3 us -> 0.23 us
    all_gather x4 -> x0, waiting for transfers between devices: 317 us -> none  [per_device(): gathered = lax.all_gather(slab_in, 'shard', axis=0, tiled=True)]
    all_to_all x0 -> x2, blocking collectives: none -> 296 us  [per_device(): shaped = lax.all_to_all(z2, 'shard', 0, 0)]
    all_to_all x0 -> x2, waiting for transfers between devices: none -> 276 us  [per_device(): shaped = lax.all_to_all(z2, 'shard', 0, 0)]
    all_to_all x0 -> x2, starting transfers between devices: none -> 20.9 us  [per_device(): shaped = lax.all_to_all(z2, 'shard', 0, 0)]
    another operation x0 -> x4, local copies, waits for them, and re-layouts: none -> 8.31 us  [per_device(): z2 = jnp.stack([slab_in] * y_new, axis=0)]
  transfers between devices with their start and end apart: 7 -> 5, of which waited for: 7 -> 5; matrix products, arithmetic and copies ran while one was open for 1% -> 0% of each run, Pallas kernels for 0% -> 0%
where the time goes in v1:
time: 641 us; the launch traced here: 638 us
  blocking collectives  296 us (46%)
  waiting for transfers between devices  283 us (44%)
  starting transfers between devices  30.3 us (5%)
  local copies, waits for them, and re-layouts  23.9 us (4%)
    all_to_all x2, blocking collectives, per_device(): shaped = lax.all_to_all(z2, 'shard', 0, 0)  296 us
    all_to_all x2, waiting for transfers between devices, per_device(): shaped = lax.all_to_all(z2, 'shard', 0, 0)  276 us
    all_to_all x2, starting transfers between devices, per_device(): shaped = lax.all_to_all(z2, 'shard', 0, 0)  20.9 us
    gather x4, local copies, waits for them, and re-layouts, propagate(): source = blocks[block_ids]  14.2 us
  transfers between devices with their start and end apart: 5, of which 5 were waited for; matrix products, arithmetic and copies ran while one was open for 0% of the time, Pallas kernels for 0%

profile of v1, /device:TPU:3, one launch (start us, length us, event | category | flops | bytes accessed | tf_op | source)
XLA Modules:
  0.0 638.4 jit_solution(2035338817429019670)
XLA Ops:
  0.0 0.0 copy-start
  0.0 3.4 stack.8
  3.4 0.0 copy-start.7
  3.4 0.0 copy-start.8
  3.4 0.0 copy-start.6
  3.4 12.6 %all-to-all-start = ((bf16[64,64,768]{2,1,0:T(8,128)(2,1)}), bf16[64,64,768]{2,1,0:T(8,128)(2,1)}, u32[]{:S(2)}, u32[]{:S(2)}) async-start(bf16[64,64,768]{2,1,0:T(8,128)(2,1)} %stack.8), calls=%async_computation | async-start | bytes 12582912 | tf_op jit(solution)/shard_map/all_to_all | solution.py:41
  16.1 0.0 copy-done.7
  16.1 0.6 constant_dynamic-slice_fusion
  16.7 0.0 copy-done
  16.7 0.2 dynamic-slice_reduce_fusion
  16.9 0.7 compare_convert_fusion
  17.5 0.0 copy-done.8
  17.6 0.0 copy-done.6
  17.6 0.1 bitcast_multiply_fusion
  17.7 137.3 %all-to-all-done = bf16[64,64,768]{2,1,0:T(8,128)(2,1)} async-done(((bf16[64,64,768]{2,1,0:T(8,128)(2,1)}), bf16[64,64,768]{2,1,0:T(8,128)(2,1)}, u32[]{:S(2)}, u32[]{:S(2)}) %all-to-all-start) | async-done | bytes 6291488 | tf_op jit(solution)/shard_map/all_to_all | solution.py:41
  154.9 3.5 gather_fusion
  158.5 0.0 copy-start.1
  158.5 0.7 fusion.4
  159.1 0.0 copy-start.2
  159.1 3.1 collective-permute-start
  162.3 2.2 collective-permute-done
  164.5 0.0 copy-done.2
  164.5 0.0 copy-done.1
  164.5 0.8 stack.9
  165.3 148.6 %all_to_all.20 = bf16[64,64,768]{2,1,0:T(8,128)(2,1)} all-to-all(bf16[64,64,768]{2,1,0:T(8,128)(2,1)S(1)} %stack.9), channel_id=1, replica_groups=mesh['section'=4,'shard'=64] {'shard'}, dimensions={0} | all-to-all | bytes 12582912 | tf_op jit(solution)/shard_map/all_to_all | solution.py:41
  313.9 3.5 gather_fusion.1
  317.4 0.7 fusion.5
  318.1 0.0 copy-start.4
  318.1 3.1 collective-permute-start.1
  321.2 2.2 collective-permute-done.1
  323.4 0.0 copy-done.4
  323.5 0.8 stack.10
  324.2 147.6 %all_to_all.21 = bf16[64,64,768]{2,1,0:T(8,128)(2,1)} all-to-all(bf16[64,64,768]{2,1,0:T(8,128)(2,1)S(1)} %stack.10), channel_id=1, replica_groups=mesh['section'=4,'shard'=64] {'shard'}, dimensions={0} | all-to-all | bytes 12582912 | tf_op jit(solution)/shard_map/all_to_all | solution.py:41
  471.8 3.5 gather_fusion.2
  475.4 0.7 fusion.6
  476.0 0.0 copy-start.5
  476.0 0.6 copy-done.5
  476.7 3.1 collective-permute-start.2
  479.8 2.2 collective-permute-done.2
  482.0 3.4 stack.11
  485.4 8.3 %all-to-all-start.3 = ((bf16[64,64,768]{2,1,0:T(8,128)(2,1)}), bf16[64,64,768]{2,1,0:T(8,128)(2,1)}, u32[]{:S(2)}, u32[]{:S(2)}) async-start(bf16[64,64,768]{2,1,0:T(8,128)(2,1)} %stack.11), calls=%async_computation.3 | async-start | bytes 12582912 | tf_op jit(solution)/shard_map/all_to_all | solution.py:41
  493.7 138.9 %all-to-all-done.3 = bf16[64,64,768]{2,1,0:T(8,128)(2,1)} async-done(((bf16[64,64,768]{2,1,0:T(8,128)(2,1)}), bf16[64,64,768]{2,1,0:T(8,128)(2,1)}, u32[]{:S(2)}, u32[]{:S(2)}) %all-to-all-start.3) | async-done | bytes 6291488 | tf_op jit(solution)/shard_map/all_to_all | solution.py:41
  632.6 0.0 copy-start.3
  632.6 3.6 gather_fusion.3
  636.2 0.0 copy-done.3
  636.2 2.2 fusion.9
  (7 shorter events, 0.1 us)
Async XLA Ops:
  0.0 16.7 %copy-start = (s32[1,32,16]{1,2,0:T(8,128)S(1)}, s32[1,32,16]{1,2,0:T(8,128)}, u32[]{:S(2)}) copy-start(s32[1,32,16]{1,2,0:T(8,128)} %param.6) | copy-start | bytes 6148
  3.4 12.7 %copy-start.7 = (s32[1,32]{1,0:T(1,128)S(1)}, s32[1,32]{1,0:T(1,128)}, u32[]{:S(2)}) copy-start(s32[1,32]{1,0:T(1,128)} %param.7) | copy-start | bytes 388
  3.4 14.1 %copy-start.8 = (s32[1,64]{1,0:T(1,128)S(1)}, s32[1,64]{1,0:T(1,128)}, u32[]{:S(2)}) copy-start(s32[1,64]{1,0:T(1,128)} %param.9) | copy-start | bytes 772
  3.4 14.1 %copy-start.6 = (bf16[1,64,16,128]{3,2,1,0:T(8,128)(2,1)S(1)}, bf16[1,64,16,128]{3,2,1,0:T(8,128)(2,1)}, u32[]{:S(2)}) copy-start(bf16[1,64,16,128]{3,2,1,0:T(8,128)(2,1)} %param.8) | copy-start | bytes 786436
  3.4 151.5 %all-to-all-start = ((bf16[64,64,768]{2,1,0:T(8,128)(2,1)}), bf16[64,64,768]{2,1,0:T(8,128)(2,1)}, u32[]{:S(2)}, u32[]{:S(2)}) async-start(bf16[64,64,768]{2,1,0:T(8,128)(2,1)} %stack.8), calls=%async_computation | async-start | bytes 12582912 | tf_op jit(solution)/shard_map/all_to_all | solution.py:41
  158.5 6.0 copy-start.1
  159.1 5.4 copy-start.2
  159.1 5.4 collective-permute-start
  318.1 5.4 copy-start.4
  318.1 5.4 collective-permute-start.1
  476.0 0.6 copy-start.5
  476.7 5.3 collective-permute-start.2
  485.4 147.2 %all-to-all-start.3 = ((bf16[64,64,768]{2,1,0:T(8,128)(2,1)}), bf16[64,64,768]{2,1,0:T(8,128)(2,1)}, u32[]{:S(2)}, u32[]{:S(2)}) async-start(bf16[64,64,768]{2,1,0:T(8,128)(2,1)} %stack.11), calls=%async_computation.3 | async-start | bytes 12582912 | tf_op jit(solution)/shard_map/all_to_all | solution.py:41
  632.6 3.6 copy-start.3
